TPU v7x, 32 devices: a whole 2x2x4 slice. The times are simulated.
32 devices in a mesh: seq: 4 (over y, x), exp: 4 (over z), ffn: 2 (over core).
Axes of the slice: x: 2, y: 2, z: 4, core: 2. Of those that a mesh axis runs over, the one named last changes fastest.
Arguments:
- tokens: bfloat16 [8, 512, 768], P(('seq', 'ffn'), 'exp'), may hold values from -6 to 6
- route_ids: int32 [8, 512, 2], P(('seq', 'ffn'), 'exp'), may hold values from 0 to 15, all different within a row; in each aligned block of 128 rows (0 to 127, 128 to 255, ..., all dimensions but the last counted through in order) at most 32 rows name the same one
- w_query: bfloat16 [768, 768], P(('seq', 'exp', 'ffn')), may hold values from -0.21875 to 0.21875
- w_key: bfloat16 [768, 768], P(('seq', 'exp', 'ffn')), may hold values from -0.21875 to 0.21875
- w_value: bfloat16 [768, 768], P(('seq', 'exp', 'ffn')), may hold values from -0.21875 to 0.21875
- w_output: bfloat16 [768, 768], P(('seq', 'exp', 'ffn')), may hold values from -1.25 to 1.25
- norm_gains: bfloat16 [2, 768], P(None, ('seq', 'exp', 'ffn')), may hold values from 0.5 to 1.5
- rel_bias: bfloat16 [384], P(('seq', 'exp', 'ffn')), may hold values from -4 to 4
- router: bfloat16 [768, 16], P(('seq', 'exp', 'ffn')), may hold values from -0.21875 to 0.21875
- w_in: bfloat16 [16, 768, 3072], P(('seq', 'exp'), None, 'ffn'), may hold values from -0.21875 to 0.21875
- w_out: bfloat16 [16, 3072, 768], P(('seq', 'exp'), 'ffn'), may hold values from -0.109375 to 0.109375
- cotangent: bfloat16 [8, 512, 768], P(('seq', 'ffn'), 'exp'), may hold values from -6 to 6
Outputs:
- output: bfloat16 [8, 512, 768], P(('seq', 'ffn'), 'exp')
- grad_tokens: float32 [8, 512, 768], P(('seq', 'ffn'), 'exp')
- grad_w_query: float32 [768, 768], P(('seq', 'exp', 'ffn'))
- grad_w_key: float32 [768, 768], P(('seq', 'exp', 'ffn'))
- grad_w_value: float32 [768, 768], P(('seq', 'exp', 'ffn'))
- grad_w_output: float32 [768, 768], P(('seq', 'exp', 'ffn'))
- grad_norm_gains: float32 [2, 768], P(None, ('seq', 'exp', 'ffn'))
- grad_rel_bias: float32 [384], P(('seq', 'exp', 'ffn'))
- grad_router: float32 [768, 16], P(('seq', 'exp', 'ffn'))
- grad_w_in: float32 [16, 768, 3072], P(('seq', 'exp'), None, 'ffn')
- grad_w_out: float32 [16, 3072, 768], P(('seq', 'exp'), 'ffn')
Inputs may be any that keep to these rules, and one draw needn't show every extreme that they name: `route_ids`: each token names 2 different experts. Among the 128 tokens of one device (aligned blocks of 128 tokens of a sequence) no expert is named more than 32 times, a bound that some block reaches.
All inputs are finite; a program needn't handle non-finite values.
Results may differ from a plain program's by a relative error of at most 0.015.
Values may be sent and summed in bfloat16 or wider, within the bound.
No kernel may reach another device: no remote copies, remote signals or barrier semaphores. Data moves between devices by JAX's collectives and lax.ppermute only.
A program may use at most 192 MiB of HBM per device.

v0:
```python
import math

import jax
import jax.numpy as jnp
from jax import lax
from jax.sharding import PartitionSpec as P

H = 12
HD = 64
TOPK = 2
BUCKETS = 32


bucket_edges = list(range(17)) + [
    math.ceil(16 * 8 ** ((bucket_level - 16) / 16)) for bucket_level in range(17, 32)
]
epsilon = 1e-06


def matmul(left, right):
    return jnp.dot(left, right, preferred_element_type=jnp.float32)


def rms_forward(hidden, gain_row):
    factor = lax.rsqrt(jnp.mean(hidden * hidden, axis=1, keepdims=True) + epsilon)
    normed = hidden * factor
    return (normed, factor, normed * gain_row)


def rms_backward(grad_out, normed, factor, gain_row):
    grad_normed = grad_out * gain_row
    grad_hidden = factor * (
        grad_normed - normed * jnp.mean(grad_normed * normed, axis=1, keepdims=True)
    )
    return (grad_hidden, jnp.sum(grad_out * normed, axis=0))


def gelu(pre_act):
    return 0.5 * pre_act * (1.0 + lax.erf(pre_act * 0.7071067811865476))


def gelu_slope(pre_act):
    return (
        0.5 * (1.0 + lax.erf(pre_act * 0.7071067811865476))
        + pre_act * jnp.exp(-0.5 * pre_act * pre_act) * 0.3989422804014327
    )


def distance_table(length):
    spans = jnp.arange(length, dtype=jnp.int32)
    edges = jnp.array(bucket_edges, jnp.int32)
    return jnp.sum((spans[None, :] >= edges[:, None]).astype(jnp.int32), axis=0) - 1


def score_block(query_heads, query_pos, key_rows, key_pos, bias_group, bucket_table, factor):
    distance = query_pos[:, None] - key_pos[None, :]
    bucket = jnp.take(bucket_table, jnp.clip(distance, 0, bucket_table.shape[0] - 1), axis=0)
    rel_terms = jnp.take(bias_group, bucket, axis=1)
    scores = (
        jnp.einsum("sqhd,skhd->shqk", query_heads, key_rows, preferred_element_type=jnp.float32)
        * factor
        + rel_terms[None]
    )
    return (scores, (distance >= 0)[None, None])


def diagonal_table(grad_scores, base, bucket_table):
    summed = jnp.sum(grad_scores, axis=0)
    heads = summed.shape[0]
    rows = summed.shape[1]
    flipped = summed[:, :, ::-1]
    padded = jnp.pad(flipped, ((0, 0), (0, 0), (0, rows)))
    skewed = padded.reshape(heads, 2 * rows * rows)[:, : rows * (2 * rows - 1)].reshape(
        heads, rows, 2 * rows - 1
    )
    per_diagonal = jnp.sum(skewed, axis=1)
    offsets = base + jnp.arange(2 * rows - 1, dtype=jnp.int32) - (rows - 1)
    bucket = jnp.take(bucket_table, jnp.clip(offsets, 0, bucket_table.shape[0] - 1), axis=0)
    levels = jnp.arange(BUCKETS, dtype=jnp.int32)
    one_hot = (bucket[:, None] == levels[None, :]).astype(jnp.float32)
    return jnp.dot(per_diagonal, one_hot, precision=lax.Precision.HIGHEST)


def backward_block(
    query_heads,
    query_pos,
    grad_heads,
    log_total,
    row_dots,
    key_rows,
    value_rows,
    key_pos,
    bias_group,
    bucket_table,
    factor,
):
    scores, causal = score_block(
        query_heads, query_pos, key_rows, key_pos, bias_group, bucket_table, factor
    )
    probabilities = jnp.where(
        causal, jnp.exp(scores - jnp.transpose(log_total, (0, 2, 1))[:, :, :, None]), 0.0
    )
    grad_values = jnp.einsum(
        "shqk,sqhd->skhd",
        probabilities.astype(jnp.bfloat16),
        grad_heads,
        preferred_element_type=jnp.float32,
    )
    grad_probs = jnp.einsum(
        "sqhd,skhd->shqk", grad_heads, value_rows, preferred_element_type=jnp.float32
    )
    grad_scores = probabilities * (grad_probs - jnp.transpose(row_dots, (0, 2, 1))[:, :, :, None])
    low_grads = grad_scores.astype(jnp.bfloat16)
    grad_query = (
        jnp.einsum("shqk,skhd->sqhd", low_grads, key_rows, preferred_element_type=jnp.float32)
        * factor
    )
    grad_keys = (
        jnp.einsum("shqk,sqhd->skhd", low_grads, query_heads, preferred_element_type=jnp.float32)
        * factor
    )
    grad_table = diagonal_table(grad_scores, query_pos[0] - key_pos[0], bucket_table)
    return (grad_query, grad_keys, grad_values, grad_table)


def body(
    tokens,
    route_ids,
    w_query,
    w_key,
    w_value,
    w_output,
    norm_gains,
    rel_bias,
    router,
    w_in,
    w_out,
    cotangent,
):
    seq_count = lax.axis_size("seq")
    exp_count = lax.axis_size("exp")
    ffn_count = lax.axis_size("ffn")
    experts = seq_count * exp_count
    devices = experts * ffn_count
    tok_rows = tokens.shape[1]
    width = tokens.shape[2]
    group_heads = H // seq_count
    group_width = group_heads * HD
    capacity = 2 * tok_rows * TOPK // experts
    factor = HD ** (-0.5)
    seq_index = lax.axis_index("seq")
    exp_index = lax.axis_index("exp")
    within = jnp.arange(tok_rows, dtype=jnp.int32)
    bucket_table = distance_table(exp_count * tok_rows)

    def positions(column):
        return column * tok_rows + within

    def fetch_weights():
        return (
            lax.all_gather(w_query, ("seq", "exp", "ffn"), axis=0, tiled=True),
            lax.all_gather(w_key, ("seq", "exp", "ffn"), axis=0, tiled=True),
            lax.all_gather(w_value, ("seq", "exp", "ffn"), axis=0, tiled=True),
            lax.all_gather(w_output, ("seq", "exp", "ffn"), axis=0, tiled=True),
            lax.all_gather(norm_gains, ("seq", "exp", "ffn"), axis=1, tiled=True),
            lax.all_gather(rel_bias, ("seq", "exp", "ffn"), axis=0, tiled=True),
            lax.all_gather(router, ("seq", "exp", "ffn"), axis=0, tiled=True),
        )

    def group_table(bias_flat):
        return lax.dynamic_slice_in_dim(
            bias_flat.astype(jnp.float32).reshape(H, BUCKETS),
            seq_index * group_heads,
            group_heads,
            0,
        )

    def split_pairs(pair_block):
        return (
            pair_block[:, :, :group_width].reshape(seq_count, -1, group_heads, HD),
            pair_block[:, :, group_width:].reshape(seq_count, -1, group_heads, HD),
        )

    full_query, full_key, full_value, full_output, gains, bias_flat, full_router = fetch_weights()
    bias_group = group_table(bias_flat)
    query_pos = positions(exp_index)
    flat_in = tokens[0].astype(jnp.float32)
    normed_one, scale_one, scaled_one = rms_forward(flat_in, gains[0].astype(jnp.float32))
    input_normed = scaled_one.astype(jnp.bfloat16)
    query_tok = matmul(input_normed, full_query).astype(jnp.bfloat16)
    key_tok = matmul(input_normed, full_key).astype(jnp.bfloat16)
    value_tok = matmul(input_normed, full_value).astype(jnp.bfloat16)
    query_wide = query_tok.reshape(1, tok_rows, seq_count, group_width)
    pair_wide = jnp.concatenate(
        [
            key_tok.reshape(tok_rows, seq_count, group_width),
            value_tok.reshape(tok_rows, seq_count, group_width),
        ],
        axis=2,
    )[None]
    query_grouped, pair_grouped = (
        lax.all_to_all(query_wide, "seq", split_axis=2, concat_axis=0, tiled=True),
        lax.all_to_all(pair_wide, "seq", split_axis=2, concat_axis=0, tiled=True),
    )
    query_heads = query_grouped.reshape(seq_count, tok_rows, group_heads, HD)
    own_pairs = pair_grouped.reshape(1, seq_count, tok_rows, 2 * group_width)
    zero_heads = jnp.zeros((seq_count, tok_rows, group_heads, HD), jnp.float32)
    shard_piece = lax.all_gather(own_pairs, "exp", axis=0, tiled=True)

    def attend_advance(current, number):
        block_index = number

        def attend_compute(state):
            numerator, denominator = state
            pair_block = lax.dynamic_index_in_dim(shard_piece, number, 0, keepdims=False)
            key_rows, value_rows = split_pairs(pair_block)
            scores, causal = score_block(
                query_heads,
                query_pos,
                key_rows,
                positions(block_index),
                bias_group,
                bucket_table,
                factor,
            )
            weights = jnp.where(causal, jnp.exp(scores), 0.0)
            numerator = numerator + jnp.einsum(
                "shqk,skhd->sqhd",
                weights.astype(jnp.bfloat16),
                value_rows,
                preferred_element_type=jnp.float32,
            )
            denominator = denominator + jnp.sum(weights, axis=3)
            return (numerator, denominator)

        return (
            lax.cond(block_index <= exp_index, attend_compute, lambda state: state, current),
            None,
        )

    result_state, unused = lax.scan(
        attend_advance,
        (zero_heads, jnp.zeros((seq_count, group_heads, tok_rows), jnp.float32)),
        jnp.arange(shard_piece.shape[0]),
    )
    numerator, denominator = result_state
    total_rows = jnp.transpose(denominator, (0, 2, 1))
    attended = (numerator / total_rows[:, :, :, None]).astype(jnp.bfloat16)
    log_total = jnp.log(total_rows)
    attended_back = lax.all_to_all(
        attended.reshape(seq_count, tok_rows, 1, group_width),
        "seq",
        split_axis=0,
        concat_axis=2,
        tiled=True,
    )
    attended_tok = attended_back.reshape(tok_rows, width)
    residual = flat_in + matmul(attended_tok, full_output)
    normed_two, scale_two, scaled_two = rms_forward(residual, gains[1].astype(jnp.float32))
    moe_normed = scaled_two.astype(jnp.bfloat16)
    logits = matmul(moe_normed, full_router)
    expert_ids = route_ids[0]
    expert_range = jnp.arange(experts, dtype=jnp.int32)
    first_hot = expert_ids[:, 0:1] == expert_range[None, :]
    second_hot = expert_ids[:, 1:2] == expert_range[None, :]
    margin = jnp.sum(jnp.where(first_hot, logits, 0.0), axis=1) - jnp.sum(
        jnp.where(second_hot, logits, 0.0), axis=1
    )
    first_gate = jax.nn.sigmoid(margin)
    gate_pair = jnp.stack([first_gate, 1.0 - first_gate], axis=1)
    flat_ids = expert_ids.reshape(-1)
    assign_hot = (flat_ids[:, None] == expert_range[None, :]).astype(jnp.int32)
    slot_index = jnp.sum(assign_hot * (jnp.cumsum(assign_hot, axis=0) - assign_hot), axis=1)
    target = flat_ids * capacity + slot_index
    placement = (
        target[None, :] == jnp.arange(experts * capacity, dtype=jnp.int32)[:, None]
    ).astype(jnp.bfloat16)

    def to_experts(assigned):
        buffer = (
            matmul(placement, assigned).astype(jnp.bfloat16).reshape(experts, 1, capacity, width)
        )
        wide = jnp.broadcast_to(buffer, (experts, ffn_count, capacity, width)).reshape(
            devices, capacity, width
        )
        return lax.all_to_all(
            wide, ("seq", "exp", "ffn"), split_axis=0, concat_axis=0, tiled=True
        ).reshape(devices * capacity, width)

    def from_experts(partial_value):
        back = lax.all_to_all(
            partial_value.reshape(devices, capacity, width),
            ("seq", "exp", "ffn"),
            split_axis=0,
            concat_axis=0,
            tiled=True,
        )
        return jnp.sum(back.reshape(experts, ffn_count, capacity, width), axis=1).reshape(
            experts * capacity, width
        )

    expert_rows = to_experts(jnp.repeat(moe_normed, TOPK, axis=0))
    pre_act = matmul(expert_rows, w_in[0])
    activated = gelu(pre_act).astype(jnp.bfloat16)
    expert_out = from_experts(matmul(activated, w_out[0]))
    picked = jnp.take(expert_out, target, axis=0).reshape(tok_rows, TOPK, width)
    output = (residual + jnp.sum(gate_pair[:, :, None] * picked, axis=1)).astype(jnp.bfloat16)
    full_query, full_key, full_value, full_output, gains, bias_flat, full_router = fetch_weights()
    bias_group = group_table(bias_flat)
    grad_mix = cotangent[0].astype(jnp.float32)
    grad_gate = jnp.sum(grad_mix[:, None, :] * picked, axis=2)
    grad_picked = (
        (gate_pair[:, :, None] * grad_mix[:, None, :]).astype(jnp.bfloat16).reshape(-1, width)
    )
    grad_rows = to_experts(grad_picked)
    grad_pre = (matmul(grad_rows, w_out[0].T) * gelu_slope(pre_act)).astype(jnp.bfloat16)
    grad_w_out = matmul(activated.T, grad_rows)[None]
    grad_w_in = matmul(expert_rows.T, grad_pre)[None]
    grad_expert_in = from_experts(matmul(grad_pre, w_in[0].T))
    grad_normed_two = jnp.sum(
        jnp.take(grad_expert_in, target, axis=0).reshape(tok_rows, TOPK, width), axis=1
    )
    gate_slope = (grad_gate[:, 0] - grad_gate[:, 1]) * first_gate * (1.0 - first_gate)
    grad_logits = (
        gate_slope[:, None] * (first_hot.astype(jnp.float32) - second_hot.astype(jnp.float32))
    ).astype(jnp.bfloat16)
    grad_router = matmul(moe_normed.T, grad_logits)
    grad_normed_two = grad_normed_two + matmul(grad_logits, full_router.T)
    grad_res_norm, grad_gain_two = rms_backward(
        grad_normed_two, normed_two, scale_two, gains[1].astype(jnp.float32)
    )
    grad_residual = grad_mix + grad_res_norm
    grad_branch = grad_residual.astype(jnp.bfloat16)
    grad_w_output = matmul(attended_tok.T, grad_branch)
    grad_attended = matmul(grad_branch, full_output.T).astype(jnp.bfloat16)
    grad_heads = lax.all_to_all(
        grad_attended.reshape(1, tok_rows, seq_count, group_width),
        "seq",
        split_axis=2,
        concat_axis=0,
        tiled=True,
    ).reshape(seq_count, tok_rows, group_heads, HD)
    row_dots = jnp.sum(grad_heads.astype(jnp.float32) * attended.astype(jnp.float32), axis=3)
    zero_table = jnp.zeros((group_heads, BUCKETS), jnp.float32)
    start_grads = (
        zero_heads,
        zero_table,
        jnp.zeros((exp_count, seq_count, tok_rows, 2 * group_width), jnp.float32),
    )
    key_shard_piece = lax.all_gather(own_pairs, "exp", axis=0, tiled=True)

    def key_advance(current, number):
        block_index = number

        def key_compute(state):
            pair_block = lax.dynamic_index_in_dim(key_shard_piece, number, 0, keepdims=False)
            key_rows, value_rows = split_pairs(pair_block)
            grad_query, grad_keys, grad_values, grad_table = backward_block(
                query_heads,
                query_pos,
                grad_heads,
                log_total,
                row_dots,
                key_rows,
                value_rows,
                positions(block_index),
                bias_group,
                bucket_table,
                factor,
            )
            updated = (state[0] + grad_query, state[1] + grad_table)
            joined = jnp.concatenate(
                [
                    grad_keys.reshape(seq_count, tok_rows, group_width),
                    grad_values.reshape(seq_count, tok_rows, group_width),
                ],
                axis=2,
            )
            earlier = lax.dynamic_index_in_dim(state[2], block_index, 0, keepdims=False)
            updated = updated + (
                lax.dynamic_update_index_in_dim(state[2], earlier + joined, block_index, 0),
            )
            return updated

        return (lax.cond(block_index <= exp_index, key_compute, lambda state: state, current), None)

    result_state, unused = lax.scan(key_advance, start_grads, jnp.arange(key_shard_piece.shape[0]))
    grad_query = result_state[0]
    grad_table = result_state[1]
    pair_grads = (
        lax.psum_scatter(
            result_state[2].astype(jnp.bfloat16), "exp", scatter_dimension=0, tiled=True
        )
        .astype(jnp.float32)
        .reshape(seq_count, tok_rows, 2 * group_width)
    )
    query_back = grad_query.astype(jnp.bfloat16).reshape(seq_count, tok_rows, 1, group_width)
    pair_back = pair_grads.astype(jnp.bfloat16).reshape(seq_count, tok_rows, 1, 2 * group_width)
    query_tok_grad, pair_tok_grad = (
        lax.all_to_all(query_back, "seq", split_axis=0, concat_axis=2, tiled=True),
        lax.all_to_all(pair_back, "seq", split_axis=0, concat_axis=2, tiled=True),
    )
    grad_query_tok = query_tok_grad.reshape(tok_rows, width)
    pair_tok_grad = pair_tok_grad.reshape(tok_rows, seq_count, 2 * group_width)
    grad_key_tok = pair_tok_grad[:, :, :group_width].reshape(tok_rows, width)
    grad_value_tok = pair_tok_grad[:, :, group_width:].reshape(tok_rows, width)
    grad_w_query = matmul(input_normed.T, grad_query_tok)
    grad_w_key = matmul(input_normed.T, grad_key_tok)
    grad_w_value = matmul(input_normed.T, grad_value_tok)
    grad_normed_one = (
        matmul(grad_query_tok, full_query.T)
        + matmul(grad_key_tok, full_key.T)
        + matmul(grad_value_tok, full_value.T)
    )
    grad_in_norm, grad_gain_one = rms_backward(
        grad_normed_one, normed_one, scale_one, gains[0].astype(jnp.float32)
    )
    grad_tokens = grad_residual + grad_in_norm
    table_full = lax.dynamic_update_slice_in_dim(
        jnp.zeros((H, BUCKETS), jnp.float32), grad_table, seq_index * group_heads, 0
    ).reshape(-1)
    summed = (
        lax.psum_scatter(grad_w_query, ("seq", "exp", "ffn"), scatter_dimension=0, tiled=True),
        lax.psum_scatter(grad_w_key, ("seq", "exp", "ffn"), scatter_dimension=0, tiled=True),
        lax.psum_scatter(grad_w_value, ("seq", "exp", "ffn"), scatter_dimension=0, tiled=True),
        lax.psum_scatter(grad_w_output, ("seq", "exp", "ffn"), scatter_dimension=0, tiled=True),
        lax.psum_scatter(
            jnp.stack([grad_gain_one, grad_gain_two]),
            ("seq", "exp", "ffn"),
            scatter_dimension=1,
            tiled=True,
        ),
        lax.psum_scatter(table_full, ("seq", "exp", "ffn"), scatter_dimension=0, tiled=True),
        lax.psum_scatter(grad_router, ("seq", "exp", "ffn"), scatter_dimension=0, tiled=True),
    )
    return (
        output[None],
        grad_tokens[None],
        summed[0],
        summed[1],
        summed[2],
        summed[3],
        summed[4],
        summed[5],
        summed[6],
        grad_w_in,
        grad_w_out,
    )


def solution(mesh):
    return jax.shard_map(
        body,
        mesh=mesh,
        in_specs=(
            P(("seq", "ffn"), "exp", None),
            P(("seq", "ffn"), "exp", None),
            P(("seq", "exp", "ffn"), None),
            P(("seq", "exp", "ffn"), None),
            P(("seq", "exp", "ffn"), None),
            P(("seq", "exp", "ffn"), None),
            P(None, ("seq", "exp", "ffn")),
            P(("seq", "exp", "ffn")),
            P(("seq", "exp", "ffn"), None),
            P(("seq", "exp"), None, "ffn"),
            P(("seq", "exp"), "ffn", None),
            P(("seq", "ffn"), "exp", None),
        ),
        out_specs=(
            P(("seq", "ffn"), "exp", None),
            P(("seq", "ffn"), "exp", None),
            P(("seq", "exp", "ffn"), None),
            P(("seq", "exp", "ffn"), None),
            P(("seq", "exp", "ffn"), None),
            P(("seq", "exp", "ffn"), None),
            P(None, ("seq", "exp", "ffn")),
            P(("seq", "exp", "ffn")),
            P(("seq", "exp", "ffn"), None),
            P(("seq", "exp"), None, "ffn"),
            P(("seq", "exp"), "ffn", None),
        ),
        check_vma=False,
    )
```

profile of v0, /device:TPU:0, one launch (start us, length us, event | category | flops | bytes accessed | tf_op | source)
XLA Modules:
  0.0 2404.2 jit_solution(17075505346014044115)
XLA Ops:
  9.5 43.5 %all-gather.1 = bf16[32,24,2]{1,2,0:T(2,128)(2,1)S(1)} all-gather(bf16[1,24,2]{1,2,0:T(2,128)(2,1)} %bitcast.357), channel_id=1, replica_groups=mesh['seq'=4,'exp'=4,'ffn'=2] {'seq','exp','ffn'}, dimensions={0}, use_global_device_ids=true | all-gather | bytes 3168 | tf_op jit(solution)/shard_map/all_gather | solution.py:165
  54.2 13.7 all-gather.9.cloned.1.call-done
  69.9 54.1 %all-gather.11.cloned.1.call-done = bf16[768,768]{1,0:T(8,128)(2,1)} async-done(((bf16[24,768]{1,0:T(8,128)(2,1)}), bf16[768,768]{1,0:T(8,128)(2,1)}) %all-gather.11.cloned.1.call-update) | async-done | bytes 1179664 | tf_op jit(solution)/shard_map/all_gather | solution.py:163
  125.8 10.2 all_to_all.110
  137.8 39.1 %all-reduce.1 = bf16[384]{0:T(512)(128)(2,1)S(1)} all-reduce(bf16[384]{0:T(512)(128)(2,1)S(1)} %dynamic-update-slice), channel_id=1, replica_groups=mesh['seq'=4,'exp'=4,'ffn'=2] {'seq','exp','ffn'}, use_global_device_ids=true, to_apply=%add.1 | all-reduce | flops 384 | bytes 1536
  178.1 2.0 all-gather.13.cloned.1.call-done
  182.6 3.4 all-to-all-start.1
  186.4 31.8 %all-gather.17.cloned.1.call-done = bf16[16,1,128,1,384]{4,2,3,1,0:T(8,128)(2,1)} async-done(((bf16[4,1,128,1,384]{4,2,3,1,0:T(8,128)(2,1)}), bf16[16,1,128,1,384]{4,2,3,1,0:T(8,128)(2,1)}) %all-gather.17.cloned.1.call-update) | async-done | bytes 1572880 | tf_op jit(solution)/shard_map/all_gather | solution.py:208
  218.1 2.6 copy.140
  220.8 174.9 %while.28 = (s32[]{:T(128)}, f32[4,128,3,64]{1,3,2,0:T(8,128)S(1)}, f32[4,3,128]{2,1,0:T(4,128)S(1)}, s32[4]{0:T(128)S(1)}, s32[]{:T(128)}, /*index=5*/bf16[4,4,...) while((s32[]{:T(128)}, f32[4,128,3,64]{1,3,2,0:T(8,128)S(1)}, ...), condition=%wide.region_6.9_spmd.clone, body=%wide.region_2.8_spmd.clone.sunk | while | flops 52035848 | bytes 5797689 | solution.py:241
  222.1 169.8 %conditional.6 = ((f32[4,128,3,64]{1,3,2,0:T(8,128)S(1)}, f32[4,3,128]{2,1,0:T(4,128)S(1)})) conditional(s32[]{:T(128)} %convert_element_type.282, (f32[4,128,3,64]{1,3,2,0:T(8,128)S(1)}, f32[4,3,128]{2,1,0:T(4,128)S(1)}) %tuple.98, (s32[]{:T(128)}, bf16[4,4,128,384]{2,3,1,0:T(8,128)(2,1)}, s32[]{:T(128)}, s32[128]{0:T(128)S(1)}, ...), branch_computations={%region_3.3_spmd, %region_4.7_spmd} | conditional | flops 52035844 | bytes 5796946 | solution.py:237
  222.8 101.8 %gather_fusion = s32[16384]{0:T(1024)S(1)} fusion(s32[512]{0:T(512)S(1)} %get-tuple-element.168, s32[16384]{0:T(1024)S(1)} %fusion.17), kind=kCustom, calls=%fused_computation.clone | custom fusion | bytes 196608 | tf_op jit(solution)/shard_map/while/body/eval_jaxpr/cond/branch_1_fun/jit(_take)/gather | solution.py:57
  325.0 54.8 %gather_fusion.1 = f32[16384,3]{1,0:T(8,128)} fusion(f32[3,32]{0,1:T(8,128)S(1)} %get-tuple-element.167, s32[16384]{0:T(1024)S(1)} %bitcast_clamp_fusion), kind=kCustom, calls=%fused_computation.1.clone | custom fusion | bytes 458752 | tf_op jit(solution)/shard_map/while/body/eval_jaxpr/cond/branch_1_fun/jit(_take)/gather | solution.py:58
  379.8 6.6 copy.124
  396.4 3.6 all-to-all-start.2
  400.1 5.2 all-to-all-done.2
  405.2 1.8 multiply_reduce_fusion.5
  408.9 1.9 reshape.428
  412.3 549.9 %all_to_all.111 = bf16[32,32,768]{2,1,0:T(8,128)(2,1)S(1)} all-to-all(bf16[32,32,768]{2,1,0:T(8,128)(2,1)S(1)} %bitcast.323), channel_id=1, replica_groups=mesh['seq'=4,'exp'=4,'ffn'=2] {'seq','exp','ffn'}, dimensions={0} | all-to-all | bytes 3145728 | tf_op jit(solution)/shard_map/all_to_all | solution.py:286
  962.2 4.9 multiply_convert_fusion
  968.8 4.3 fusion.47
  973.1 3.8 all-to-all-start.4
  978.1 2.6 mul.283
  980.7 97.4 %all-gather.2 = bf16[32,24,16]{1,2,0:T(8,128)(2,1)S(1)} all-gather(bf16[1,24,16]{1,2,0:T(8,128)(2,1)S(1)} %bitcast.356), channel_id=1, replica_groups=mesh['seq'=4,'exp'=4,'ffn'=2] {'seq','exp','ffn'}, dimensions={0}, use_global_device_ids=true | all-gather | bytes 25344 | tf_op jit(solution)/shard_map/all_gather | solution.py:167
  1078.6 3.4 bitcast_reduce_fusion.1
  1082.1 3.7 gather_fusion.5
  1085.7 2.4 multiply_reduce_fusion
  1090.6 40.6 %all_to_all.112 = bf16[32,32,768]{2,1,0:T(8,128)(2,1)S(1)} all-to-all(bf16[32,32,768]{2,1,0:T(8,128)(2,1)S(1)} %bitcast.324), channel_id=1, replica_groups=mesh['seq'=4,'exp'=4,'ffn'=2] {'seq','exp','ffn'}, dimensions={0} | all-to-all | bytes 3145728 | tf_op jit(solution)/shard_map/all_to_all | solution.py:286
  1131.2 7.3 fusion.44
  1140.2 4.3 fusion.45
  1144.5 3.7 all-to-all-start.6
  1148.6 1.8 multiply_reduce_fusion.1
  1150.4 70.3 %all-to-all-done.6 = f32[32,32,768]{2,1,0:T(8,128)} async-done(((f32[32,32,768]{2,1,0:T(8,128)}), f32[32,32,768]{2,1,0:T(8,128)}, u32[]{:S(2)}, u32[]{:S(2)}) %all-to-all-start.6) | async-done | bytes 3145760 | tf_op jit(solution)/shard_map/all_to_all | solution.py:291
  1220.7 2.3 bitcast_reduce_fusion
  1226.5 1.9 multiply_add_fusion
  1229.8 3.4 all-to-all-start.7
  1233.4 4.9 all-to-all-done.7
  1238.4 2.0 broadcast_in_dim.148
  1240.4 179.6 %while.29 = (s32[]{:T(128)}, f32[4,128,3,64]{1,3,2,0:T(8,128)S(1)}, f32[3,32]{1,0:T(4,128)S(1)}, f32[4,4,128,384]{2,3,1,0:T(8,128)}, s32[4]{0:T(128)S(1)}, /*ind...) while((s32[]{:T(128)}, f32[4,128,3,64]{1,3,2,0:T(8,128)S(1)}, ...), condition=%wide.region_25.29_spmd.clone, body=%wide.region_20.28_spmd.clone.sunk | while | flops 129264688 | bytes 16807020 | solution.py:387
  1241.7 174.5 %conditional.7 = ((f32[4,128,3,64]{1,3,2,0:T(8,128)S(1)}, f32[3,32]{1,0:T(4,128)S(1)}, f32[4,4,128,384]{2,3,1,0:T(8,128)})) conditional(s32[]{:T(128)} %convert_element_type.283, (f32[4,128,3,64]{1,3,2,0:T(8,128)S(1)}, f32[3,32]{1,0:T(4,128)S(1)}, f32[4,4,128,384]{2,3,1,0:T(8,128)}) %tuple.101, (s32[]{:T(128)}, ...), branch_computations={%region_21.24_spmd, %region_22.27_spmd} | conditional | flops 129264688 | bytes 16806206 | solution.py:385
  1242.5 101.8 %gather_fusion.3 = s32[16384]{0:T(1024)S(1)} fusion(s32[512]{0:T(512)S(1)} %get-tuple-element.191, s32[16384]{0:T(1024)S(1)} %fusion.36), kind=kCustom, calls=%fused_computation.3.clone | custom fusion | bytes 196608 | tf_op jit(solution)/shard_map/while/body/eval_jaxpr/cond/branch_1_fun/jit(_take)/gather | solution.py:57
  1344.6 54.5 %gather_fusion.4 = f32[16384,3]{1,0:T(8,128)} fusion(f32[3,32]{0,1:T(8,128)S(1)} %get-tuple-element.190, s32[16384]{0:T(1024)S(1)} %bitcast_clamp_fusion.1), kind=kCustom, calls=%fused_computation.4.clone | custom fusion | bytes 458752 | tf_op jit(solution)/shard_map/while/body/eval_jaxpr/cond/branch_1_fun/jit(_take)/gather | solution.py:58
  1399.1 6.6 copy.128
  1410.3 2.1 fusion.28
  1413.7 1.9 gather_fusion.2
  1420.1 3.4 convert_element_type.168
  1423.6 1.9 fusion.73
  1425.6 7.9 all_to_all.113
  1433.5 2.1 fusion.93
  1435.7 543.4 %reduce-scatter.8.cloned.1.call-done = bf16[1,4,128,384]{2,3,1,0:T(8,128)(2,1)} async-done(((bf16[4,4,128,384]{2,3,1,0:T(8,128)(2,1)}), bf16[1,4,128,384]{2,3,1,0:T(8,128)(2,1)}) %reduce-scatter.8.cloned.1.call-update) | async-done | bytes 393232 | tf_op jit(solution)/shard_map/reduce_scatter | solution.py:391
  1979.1 10.5 all_to_all.114
  1989.6 2.0 fusion.91
  1992.0 2.0 fusion.89
  1994.2 7.4 convolution_bitcast_fusion.1
  2001.6 4.3 convolution_bitcast_fusion.2
  2006.2 1.8 fusion.104
  2008.0 2.1 convolution_add_fusion.2
  2010.1 2.6 fusion.64
  2012.7 39.5 %all-reduce.5 = (f32[2,768]{1,0:T(2,128)S(1)}, f32[384]{0:T(512)S(1)}, f32[768,16]{0,1:T(8,128)S(1)}) all-reduce(f32[2,768]{1,0:T(2,128)S(1)} %pad_maximum_fusion, f32[384]{0:T(512)S(1)} %reshape.446, f32[768,16]{0,1:T(8,128)S(1)} %fusion.80), channel_id=8, replica_groups=mesh['seq'=4,'exp'=4,'ffn'=2] {'seq','exp','ffn'}, use_global_device_ids=true, to_apply=%region_34.38.clone | all-reduce | flops 14208 | bytes 113664
  2054.1 1.9 fusion.63
  2056.1 27.4 %reduce-scatter.16.cloned.1.call-done = f32[24,768]{1,0:T(8,128)} async-done(((f32[768,768]{1,0:T(8,128)}), f32[24,768]{1,0:T(8,128)}) %reduce-scatter.16.cloned.1.call-update) | async-done | bytes 73744 | tf_op jit(solution)/shard_map/reduce_scatter | solution.py:426
  2083.5 104.5 %reduce-scatter.10.cloned.1.call-done = f32[24,768]{1,0:T(8,128)} async-done(((f32[768,768]{1,0:T(8,128)}), f32[24,768]{1,0:T(8,128)}) %reduce-scatter.10.cloned.1.call-update) | async-done | bytes 73744 | tf_op jit(solution)/shard_map/reduce_scatter | solution.py:423
  2188.0 104.5 %reduce-scatter.12.cloned.1.call-done = f32[24,768]{1,0:T(8,128)} async-done(((f32[768,768]{1,0:T(8,128)}), f32[24,768]{1,0:T(8,128)}) %reduce-scatter.12.cloned.1.call-update) | async-done | bytes 73744 | tf_op jit(solution)/shard_map/reduce_scatter | solution.py:424
  2292.5 104.4 %reduce-scatter.14.cloned.1.call-done = f32[24,768]{1,0:T(8,128)} async-done(((f32[768,768]{1,0:T(8,128)}), f32[24,768]{1,0:T(8,128)}) %reduce-scatter.14.cloned.1.call-update) | async-done | bytes 73744 | tf_op jit(solution)/shard_map/reduce_scatter | solution.py:425
  (237 shorter events, 46.6 us)
Async XLA Ops:
  7.2 955.1 %copy-start = (bf16[1,768,1536]{2,1,0:T(8,128)(2,1)S(1)}, bf16[1,768,1536]{2,1,0:T(8,128)(2,1)}, u32[]{:S(2)}) copy-start(bf16[1,768,1536]{2,1,0:T(8,128)(2,1)} %param.36) | copy-start | bytes 7077892
  7.2 116.8 %copy-start.2 = (bf16[1,128,768]{2,1,0:T(8,128)(2,1)S(1)}, bf16[1,128,768]{2,1,0:T(8,128)(2,1)}, u32[]{:S(2)}) copy-start(bf16[1,128,768]{2,1,0:T(8,128)(2,1)} %param.27) | copy-start | bytes 589828
  7.2 60.7 %all-gather.9.cloned.1.call-start = ((), (), s32[]{:S(2)}) async-start(), calls=%async_computation.15 | async-start | bytes 1216512 | tf_op jit(solution)/shard_map/all_gather | solution.py:162
  7.9 116.0 %all-gather.11.cloned.1.call-start = ((), (), s32[]{:S(2)}) async-start(), calls=%async_computation.16 | async-start | bytes 1216512 | tf_op jit(solution)/shard_map/all_gather | solution.py:163
  8.7 171.4 %all-gather.13.cloned.1.call-start = ((), (), s32[]{:S(2)}) async-start(), calls=%async_computation.17 | async-start | bytes 1216512 | tf_op jit(solution)/shard_map/all_gather | solution.py:161
  9.4 208.7 %all-gather.17.cloned.1.call-start = ((), (), s32[]{:S(2)}) async-start(), calls=%async_computation.24 | async-start | bytes 1966080 | tf_op jit(solution)/shard_map/all_gather | solution.py:208
  53.1 127.0 %copy-start.23 = (f32[768]{0:T(1024)}, f32[768]{0:T(1024)S(1)}, u32[]{:S(2)}) copy-start(f32[768]{0:T(1024)S(1)} %get-tuple-element.407) | copy-start | bytes 9220
  54.2 126.0 %copy-start.25 = (f32[128]{0:T(128)}, f32[128]{0:T(128)S(1)}, u32[]{:S(2)}) copy-start(f32[128]{0:T(128)S(1)} %add_rsqrt_fusion.1) | copy-start | bytes 1540
  69.8 67.7 %copy-start.33 = (bf16[12]{0:T(256)(128)(2,1)S(1)}, bf16[12]{0:T(256)(128)(2,1)}, u32[]{:S(2)}) copy-start(bf16[12]{0:T(256)(128)(2,1)} %param.34) | copy-start | bytes 76
  69.8 107.1 %copy-start.28 = (s32[1,128,2]{1,2,0:T(2,128)S(1)}, s32[1,128,2]{1,2,0:T(2,128)}, u32[]{:S(2)}) copy-start(s32[1,128,2]{1,2,0:T(2,128)} %param.28) | copy-start | bytes 3076
  69.8 108.2 %copy-start.30 = (s32[32]{0:T(128)S(1)}, s32[32]{0:T(128)}, u32[]{:S(2)}) copy-start(s32[32]{0:T(128)} %constant.149.clone) | copy-start | bytes 388
  136.9 263.1 %all-gather.15.cloned.1.call-start = ((), (), s32[]{:S(2)}) async-start(), calls=%async_computation.18 | async-start | bytes 1216512 | tf_op jit(solution)/shard_map/all_gather | solution.py:164
  182.6 38.1 %all-to-all-start.1 = ((bf16[1,128,4,192]{1,3,0,2:T(8,128)(2,1)}), bf16[1,128,4,192]{1,3,0,2:T(8,128)(2,1)S(1)}, u32[]{:S(2)}, u32[]{:S(2)}) async-start(bf16[1,128,4,192]{1,3,0,2:T(8,128)(2,1)} %bitcast.41), calls=%async_computation.1 | async-start | bytes 393216 | tf_op jit(solution)/shard_map/all_to_all | solution.py:202
  396.4 8.8 all-to-all-start.2
  405.2 6.9 copy-start.16
  407.0 0.8 copy-start.8
  407.9 670.5 %copy-start.14 = (bf16[128,768]{1,0:T(8,128)(2,1)}, bf16[128,768]{1,0:T(8,128)(2,1)S(1)}, u32[]{:S(2)}) copy-start(bf16[128,768]{1,0:T(8,128)(2,1)S(1)} %multiply_convert_fusion.3) | copy-start | bytes 589828
  962.2 4.9 copy-start.4
  962.2 6.6 copy-start.31
  967.1 1.7 copy-start.34
  973.1 3.9 copy-start.22
  973.1 105.5 %all-to-all-start.4 = ((f32[32,32,768]{2,1,0:T(8,128)}), f32[32,32,768]{2,1,0:T(8,128)}, u32[]{:S(2)}, u32[]{:S(2)}) async-start(f32[32,32,768]{2,1,0:T(8,128)} %fusion.47), calls=%async_computation.4 | async-start | bytes 6291456 | tf_op jit(solution)/shard_map/all_to_all | solution.py:291
  976.9 3.8 copy-start.29
  1090.4 40.8 %copy-start.32 = (bf16[1,1536,768]{2,1,0:T(8,128)(2,1)S(1)}, bf16[1,1536,768]{2,1,0:T(8,128)(2,1)}, u32[]{:S(2)}) copy-start(bf16[1,1536,768]{2,1,0:T(8,128)(2,1)} %param.37) | copy-start | bytes 7077892
  1131.2 7.3 copy-start.21
  1138.5 1.7 copy-start.12
  1144.5 3.7 copy-start.11
  1144.5 76.2 %all-to-all-start.6 = ((f32[32,32,768]{2,1,0:T(8,128)}), f32[32,32,768]{2,1,0:T(8,128)}, u32[]{:S(2)}, u32[]{:S(2)}) async-start(f32[32,32,768]{2,1,0:T(8,128)} %fusion.45), calls=%async_computation.6 | async-start | bytes 6291456 | tf_op jit(solution)/shard_map/all_to_all | solution.py:291
  1224.1 1.6 copy-start.9
  1224.7 3.7 copy-start.10
  1228.4 10.0 copy-start.6
  1229.8 8.5 all-to-all-start.7
  1233.1 746.0 %reduce-scatter.8.cloned.1.call-start = ((), (), s32[]{:S(2)}) async-start(), calls=%async_computation.19 | async-start | bytes 1966080 | tf_op jit(solution)/shard_map/reduce_scatter | solution.py:391
  1420.1 3.5 copy-start.7
  1420.1 3.5 copy-start.17
  1423.6 660.0 %reduce-scatter.16.cloned.1.call-start = ((), (), s32[]{:S(2)}) async-start(), calls=%async_computation.23 | async-start | bytes 2433024 | tf_op jit(solution)/shard_map/reduce_scatter | solution.py:426
  1425.5 8.0 copy-start.3
  1425.5 8.0 copy-start.24
  1425.5 8.0 copy-start.26
  1425.5 762.5 %reduce-scatter.10.cloned.1.call-start = ((), (), s32[]{:S(2)}) async-start(), calls=%async_computation.20 | async-start | bytes 2433024 | tf_op jit(solution)/shard_map/reduce_scatter | solution.py:423
  1435.6 856.9 %reduce-scatter.12.cloned.1.call-start = ((), (), s32[]{:S(2)}) async-start(), calls=%async_computation.21 | async-start | bytes 2433024 | tf_op jit(solution)/shard_map/reduce_scatter | solution.py:424
  1989.6 2.0 copy-start.20
  1989.6 2.4 copy-start.18
  1991.7 405.2 %reduce-scatter.14.cloned.1.call-start = ((), (), s32[]{:S(2)}) async-start(), calls=%async_computation.22 | async-start | bytes 2433024 | tf_op jit(solution)/shard_map/reduce_scatter | solution.py:425
  1992.0 2.0 copy-start.15
  1994.2 7.5 copy-start.5
  1994.2 7.4 copy-start.13
  2001.6 4.3 copy-start.27
  2005.9 4.2 copy-start.19
  2008.0 388.9 %copy-start.1 = (bf16[1,768,1536]{2,1,0:T(8,128)(2,1)S(1)}, bf16[1,768,1536]{2,1,0:T(8,128)(2,1)}, u32[]{:S(2)}) copy-start(bf16[1,768,1536]{2,1,0:T(8,128)(2,1)} %param.36) | copy-start | bytes 7077892
Sparse Core Ops, SparseCore 0:
  11.0 56.8 all-gather.8
  70.9 52.9 all-gather.10
  127.0 53.1 all-gather.12
  182.1 35.9 all-gather.16
  221.0 52.9 all-gather.14
  1423.7 555.4 reduce-scatter.7
  1985.0 98.4 reduce-scatter.15
  2089.4 98.5 reduce-scatter.9
  2193.9 98.5 reduce-scatter.11
  2298.2 98.6 reduce-scatter.13
where the time goes:
time: 2410 us; the launch traced here: 2400 us
  waiting for transfers between devices  1070 us (44%)
  blocking collectives  839 us (35%)
  local copies, waits for them, and re-layouts  365 us (15%)
  matrix products  61.9 us (3%)
  other arithmetic  24.7 us (1%)
    all_to_all x2, blocking collectives, to_experts(): lax.all_to_all(wide, ('seq', 'exp', 'ffn'), split_axis=0, concat_axis=0,...  590 us
    reduce_scatter x1, waiting for transfers between devices, body(): lax.psum_scatter(result_state[2].astype(jnp.bfloat16), 'exp', scatter_dim...  543 us
    gather x2, local copies, waits for them, and re-layouts, score_block(): jnp.take(bucket_table, jnp.clip(distance, 0, bucket_table.shape[0] - 1),...  204 us
    gather x4, local copies, waits for them, and re-layouts, score_block(): rel_terms = jnp.take(bias_group, bucket, axis=1)  122 us
    reduce_scatter x1, waiting for transfers between devices, body(): lax.psum_scatter(grad_w_key, ('seq', 'exp', 'ffn'), scatter_dimension=0,...  104 us
    reduce_scatter x1, waiting for transfers between devices, body(): lax.psum_scatter(grad_w_query, ('seq', 'exp', 'ffn'), scatter_dimension=0...  104 us
    reduce_scatter x1, waiting for transfers between devices, body(): lax.psum_scatter(grad_w_value, ('seq', 'exp', 'ffn'), scatter_dimension=0...  104 us
    all_gather x1, blocking collectives, fetch_weights(): lax.all_gather(router, ('seq', 'exp', 'ffn'), axis=0, tiled=True)  97.4 us
  transfers between devices with their start and end apart: 15, of which 12 were waited for; matrix products, arithmetic and copies ran while one was open for 9% of the time, Pallas kernels for 0%

commit v1 on v0

v1 whole, which is shorter than its diff:
```python
import functools
import math

import jax
import jax.numpy as jnp
import numpy as np
from jax import lax
from jax.experimental import pallas as pl
from jax.experimental.pallas import tpu as pltpu
from jax.sharding import PartitionSpec as P

H = 12
HD = 64
TOPK = 2
BUCKETS = 32
LANES = 128

bucket_edges = list(range(17)) + [
    math.ceil(16 * 8 ** ((bucket_level - 16) / 16)) for bucket_level in range(17, 32)
]
epsilon = 1e-06
scale = HD ** (-0.5)
f32 = jnp.float32
bf16 = jnp.bfloat16
EXACT = lax.Precision.HIGHEST


def dot(left, right, left_dim=1, right_dim=0, precision=None):
    return lax.dot_general(
        left,
        right,
        (((left_dim,), (right_dim,)), ((), ())),
        precision=precision,
        preferred_element_type=f32,
    )


def mean_rows(values):
    return jnp.mean(values, axis=1, keepdims=True)


def iota(shape, axis):
    return lax.broadcasted_iota(jnp.int32, shape, axis)


def rms_factor(hidden):
    return lax.rsqrt(mean_rows(hidden * hidden) + epsilon)


def rms_backward(grad_out, normed, factor, gain_row):
    grad_normed = grad_out * gain_row
    return factor * (grad_normed - normed * mean_rows(grad_normed * normed))


def shear(tile, leftward):
    rows = iota(tile.shape, 0)
    for bit in range(7):
        step = 1 << bit
        moved = pltpu.roll(tile, LANES - step if leftward else step, axis=1)
        tile = jnp.where((rows & step) != 0, moved, tile)
    return tile


class Plan:
    def __init__(self, tok, width, hidden):
        self.seq = lax.axis_size("seq")
        self.exp = lax.axis_size("exp")
        self.ffn = lax.axis_size("ffn")
        self.experts = self.seq * self.exp
        self.devices = self.experts * self.ffn
        self.tok = tok
        self.width = width
        self.hidden = hidden
        self.groups = math.gcd(H, self.exp)
        self.copies = self.exp // self.groups
        self.gh = H // self.groups
        self.gw = self.gh * HD
        self.length = self.exp * tok
        self.queries = self.length // self.copies
        self.blocks = self.exp // self.copies
        self.cap = 2 * tok * TOPK // self.experts
        self.slots = self.experts * self.cap
        self.shard = width // self.devices
        self.bias_shard = H * BUCKETS // self.devices
        self.extra = self.experts + 3
        self.qkv = 3 * self.gw
        self.packed = -(-(self.qkv + self.extra) // LANES) * LANES
        self.chunk = LANES * max(1, -(-(2 * self.extra) // LANES))
        self.first = self.packed - self.chunk
        self.off = self.qkv - self.first
        assert self.first % self.chunk == 0 and 0 <= self.off
        assert self.off + self.extra <= self.chunk
        assert tok == LANES and bucket_edges[-1] <= LANES

    def selectors(self):
        head = np.zeros((16, self.width), np.float32)
        spread = np.zeros((self.width, LANES), np.float32)
        distance = (-np.arange(LANES)) % LANES
        bucket = (distance[:, None] >= np.array(bucket_edges)[None, :]).sum(1) - 1
        for device in range(self.devices):
            for place in range(self.bias_shard):
                row = device * self.shard + place
                flat = device * self.bias_shard + place
                head[flat // BUCKETS, row] = 1.0
                spread[row] = bucket == flat % BUCKETS
        return jnp.asarray(head, bf16), jnp.asarray(spread, bf16)


def whole(shape, memory_space=pltpu.VMEM):
    zeros = (0,) * len(shape)
    return pl.BlockSpec(shape, lambda step: zeros, memory_space=memory_space)


def chunk_spec(plan):
    index = plan.first // plan.chunk
    return pl.BlockSpec((plan.width, plan.chunk), lambda step: (0, index), memory_space=pltpu.VMEM)


def bias_tile(table_ref, head):
    row = table_ref[pl.ds(head, 1), :]
    far = row[:, 1:2]
    return shear(jnp.broadcast_to(row, (LANES, LANES)), False), far


def score_rows(plan, qkv_ref, head, query, base, keys, tile, far):
    lanes = head * HD
    query_rows = qkv_ref[pl.ds(query, LANES), lanes : lanes + HD]
    key_rows = qkv_ref[0:keys, plan.gw + lanes : plan.gw + lanes + HD]
    value_rows = qkv_ref[0:keys, 2 * plan.gw + lanes : 2 * plan.gw + lanes + HD]
    distance = base + iota((LANES, keys), 0) - iota((LANES, keys), 1)
    bias = jnp.where(distance >= LANES, far, jnp.concatenate([tile] * (keys // LANES), axis=1))
    scores = dot(query_rows, key_rows, 1, 1) * scale + bias
    return scores, distance, query_rows, key_rows, value_rows


def first_query(plan):
    if plan.copies == 1:
        return 0
    return (lax.axis_index("exp") % plan.copies) * plan.queries


def first_head(plan):
    return (lax.axis_index("exp") // plan.copies) * plan.gh


def query_blocks(plan):
    start = first_query(plan)
    for block in range(plan.blocks):
        local = block * LANES
        keys = local + LANES if plan.copies == 1 else plan.length
        at = start + local
        if plan.copies > 1:
            at = pl.multiple_of(at, LANES)
        yield local, at, keys


def attend_kernel(plan, x_ref, wp_ref, head_ref, spread_ref, att_ref, qkv_ref, lse_ref, table_ref):
    extra = wp_ref[:, plan.first : plan.packed].astype(f32)
    place = plan.off + plan.experts
    gain = jnp.transpose(extra)[place : place + 1, :]
    bias_column = extra[:, place + 2 : place + 3]
    table_ref[...] = dot(head_ref[...], (bias_column * spread_ref[...].astype(f32)).astype(bf16))
    hidden = x_ref[...].astype(f32)
    normed = hidden * rms_factor(hidden)
    scaled = (normed * gain).astype(bf16)
    qkv_ref[...] = dot(scaled, wp_ref[:, 0 : plan.qkv]).astype(bf16)
    lse_ref[...] = jnp.zeros_like(lse_ref)
    for head in range(plan.gh):
        tile, far = bias_tile(table_ref, first_head(plan) + head)
        for local, at, keys in query_blocks(plan):
            scores, distance, _, _, value_rows = score_rows(
                plan, qkv_ref, head, at, at, keys, tile, far
            )
            weights = jnp.where(distance >= 0, jnp.exp(scores), 0.0)
            total = jnp.sum(weights, axis=1, keepdims=True)
            numerator = dot(weights.astype(bf16), value_rows)
            att_ref[local : local + LANES, head * HD : (head + 1) * HD] = (
                numerator / total
            ).astype(bf16)
            lse_ref[local : local + LANES, head : head + 1] = jnp.log(total)


def routing(plan, ids_ref):
    lane = iota((plan.tok, plan.chunk), 1) - plan.off
    first_hot = lane == ids_ref[:, 0:1]
    second_hot = lane == ids_ref[:, 1:2]
    return first_hot, second_hot


def pick(hot, values):
    return jnp.sum(jnp.where(hot, values, 0.0), axis=1, keepdims=True)


def placements(plan, meta):
    slot = iota((plan.tok, plan.slots), 1).astype(f32)
    return (
        (slot == meta[:, 1:2]).astype(f32).astype(bf16),
        (slot == meta[:, 2:3]).astype(f32).astype(bf16),
    )


def middle_kernel(
    plan, att_ref, wo_ref, x_ref, cot_ref, ids_ref, chunk_ref, send_ref, res_ref, meta_ref, atok_ref
):
    for group in range(plan.groups):
        atok_ref[:, group * plan.gw : (group + 1) * plan.gw] = att_ref[group]
    residual = x_ref[...].astype(f32) + dot(atok_ref[...], wo_ref[...])
    res_ref[...] = residual
    chunk = chunk_ref[...]
    place = plan.off + plan.experts + 1
    gain = jnp.transpose(chunk.astype(f32))[place : place + 1, :]
    normed = residual * rms_factor(residual)
    moe_normed = (normed * gain).astype(bf16)
    logits = dot(moe_normed, chunk)
    first_hot, second_hot = routing(plan, ids_ref)
    margin = pick(first_hot, logits) - pick(second_hot, logits)
    first_gate = 1.0 / (1.0 + jnp.exp(-margin))
    named = jnp.logical_or(first_hot, second_hot).astype(f32).astype(bf16)
    earlier = (iota((plan.tok, plan.tok), 0) > iota((plan.tok, plan.tok), 1)).astype(f32)
    counts = dot(earlier.astype(bf16), named)
    ids = ids_ref[...].astype(f32) * float(plan.cap)
    meta_lane = iota((plan.tok, LANES), 1)
    meta = jnp.where(
        meta_lane == 0,
        first_gate,
        jnp.where(
            meta_lane == 1,
            ids[:, 0:1] + pick(first_hot, counts),
            jnp.where(meta_lane == 2, ids[:, 1:2] + pick(second_hot, counts), 0.0),
        ),
    )
    meta_ref[...] = meta
    first_place, second_place = placements(plan, meta)
    cot = cot_ref[...].astype(f32)
    first_grad = (first_gate * cot).astype(bf16)
    second_grad = ((1.0 - first_gate) * cot).astype(bf16)
    send_ref[:, 0 : plan.width] = dot(first_place + second_place, moe_normed, 0, 0).astype(bf16)
    send_ref[:, plan.width :] = (
        dot(first_place, first_grad, 0, 0) + dot(second_place, second_grad, 0, 0)
    ).astype(bf16)


def expert_kernel(
    plan, own_ref, other_ref, win_ref, wout_ref, mine_ref, theirs_ref, gin_ref, gout_ref, rows_ref, acc_ref
):
    step = pl.program_id(0)
    half = own_ref.shape[0]
    width = plan.width

    @pl.when(step == 0)
    def _():
        rows_ref[0:half, :] = own_ref[...]
        rows_ref[half:, :] = other_ref[...]
        acc_ref[...] = jnp.zeros_like(acc_ref)

    rows = rows_ref[:, 0:width]
    grads = rows_ref[:, width:]
    w_in = win_ref[0]
    w_out = wout_ref[0]
    pre_act = dot(rows, w_in)
    phi = 0.5 * (1.0 + lax.erf(pre_act * 0.7071067811865476))
    activated = (pre_act * phi).astype(bf16)
    slope = phi + pre_act * jnp.exp(-0.5 * pre_act * pre_act) * 0.3989422804014327
    grad_pre = (dot(grads, w_out, 1, 1) * slope).astype(bf16)
    acc_ref[:, 0:width] += dot(activated, w_out)
    acc_ref[:, width:] += dot(grad_pre, w_in, 1, 1)
    gout_ref[0] = dot(activated, grads, 0, 0)
    gin_ref[0] = dot(rows, grad_pre, 0, 0)

    @pl.when(step == pl.num_programs(0) - 1)
    def _():
        mine_ref[...] = acc_ref[0:half, :]
        theirs_ref[...] = acc_ref[half:, :].astype(bf16)


def combine_kernel(
    plan, back_ref, meta_ref, res_ref, cot_ref, ids_ref, chunk_ref, wo_ref, atok_ref,
    out_ref, gres_ref, gatt_ref, gwo_ref, small_ref,
):
    width = plan.width
    meta = meta_ref[...]
    first_gate = meta[:, 0:1]
    first_place, second_place = placements(plan, meta)
    back = back_ref[...]
    first = dot(first_place, back)
    second = dot(second_place, back)
    residual = res_ref[...]
    out_ref[...] = (
        residual + (first_gate * first[:, 0:width] + (1.0 - first_gate) * second[:, 0:width])
    ).astype(bf16)
    cot = cot_ref[...].astype(f32)
    grad_gate = jnp.sum(cot * first[:, 0:width], axis=1, keepdims=True) - jnp.sum(
        cot * second[:, 0:width], axis=1, keepdims=True
    )
    gate_slope = grad_gate * first_gate * (1.0 - first_gate)
    first_hot, second_hot = routing(plan, ids_ref)
    grad_logits = (
        gate_slope * (first_hot.astype(f32) - second_hot.astype(f32))
    ).astype(bf16)
    chunk = chunk_ref[...]
    place = plan.off + plan.experts + 1
    gain = jnp.transpose(chunk.astype(f32))[place : place + 1, :]
    factor = rms_factor(residual)
    normed = residual * factor
    moe_normed = (normed * gain).astype(bf16)
    grad_normed = first[:, width:] + second[:, width:] + dot(grad_logits, chunk, 1, 1)
    grad_residual = cot + rms_backward(grad_normed, normed, factor, gain)
    gres_ref[...] = grad_residual
    grad_branch = grad_residual.astype(bf16)
    grad_attended = dot(grad_branch, wo_ref[...], 1, 1).astype(bf16)
    for group in range(plan.groups):
        gatt_ref[group] = grad_attended[:, group * plan.gw : (group + 1) * plan.gw]
    gwo_ref[...] = dot(atok_ref[...], grad_branch, 0, 0).astype(bf16)
    grad_router = dot(moe_normed, grad_logits, 0, 0)
    grad_gain = jnp.sum(grad_normed * normed, axis=0, keepdims=True)
    columns = jnp.transpose(jnp.broadcast_to(grad_gain, (plan.chunk, width)))
    lane = iota((width, plan.chunk), 1)
    small_ref[...] = jnp.where(
        lane == place, columns, jnp.where(lane < plan.off, 0.0, grad_router)
    )


def backward_kernel(
    plan, x_ref, wp_ref, head_ref, spread_ref, qkv_ref, att_ref, gatt_ref, lse_ref, table_ref, part_ref,
    gx_ref, gw_ref, small_ref, pair_ref, grad_ref, sums_ref,
):
    extra = wp_ref[:, plan.first : plan.packed].astype(f32)
    place = plan.off + plan.experts
    gain = jnp.transpose(extra)[place : place + 1, :]
    pair_ref[...] = jnp.zeros_like(pair_ref)
    sums_ref[...] = jnp.zeros_like(sums_ref)
    if plan.copies > 1:
        grad_ref[...] = jnp.zeros_like(grad_ref)
    for head in range(plan.gh):
        lanes = head * HD
        tile, far = bias_tile(table_ref, first_head(plan) + head)
        near_sum = jnp.zeros((LANES, LANES), f32)
        far_sum = jnp.zeros((1, LANES), f32)
        for local, at, keys in query_blocks(plan):
            scores, distance, query_rows, key_rows, value_rows = score_rows(
                plan, qkv_ref, head, at, at, keys, tile, far
            )
            log_total = lse_ref[local : local + LANES, head : head + 1]
            weights = jnp.where(distance >= 0, jnp.exp(scores - log_total), 0.0)
            grads = gatt_ref[local : local + LANES, lanes : lanes + HD]
            attended = att_ref[local : local + LANES, lanes : lanes + HD]
            row_dots = jnp.sum(grads.astype(f32) * attended.astype(f32), axis=1, keepdims=True)
            grad_scores = weights * (dot(grads, value_rows, 1, 1) - row_dots)
            low = grad_scores.astype(bf16)
            near = jnp.where(distance < LANES, grad_scores, 0.0)
            rest = jnp.sum(jnp.where(distance < LANES, 0.0, grad_scores), axis=0, keepdims=True)
            for part in range(keys // LANES):
                near_sum = near_sum + near[:, part * LANES : (part + 1) * LANES]
                far_sum = far_sum + rest[:, part * LANES : (part + 1) * LANES]
            grad_ref[pl.ds(at, LANES), lanes : lanes + HD] = (dot(low, key_rows) * scale).astype(
                bf16
            )
            pair_ref[0:keys, lanes : lanes + HD] += dot(low, query_rows, 0, 0) * scale
            pair_ref[0:keys, plan.gw + lanes : plan.gw + lanes + HD] += dot(
                weights.astype(bf16), grads, 0, 0
            )
        by_distance = jnp.sum(shear(near_sum, True), axis=0, keepdims=True)
        by_distance = by_distance + jnp.where(
            iota((1, LANES), 1) == 1, jnp.sum(far_sum, axis=1, keepdims=True), 0.0
        )
        sums_ref[pl.ds(first_head(plan) + head, 1), :] = by_distance
    grad_ref[:, plan.gw :] = pair_ref[...].astype(bf16)
    hidden = x_ref[...].astype(f32)
    normed = hidden * rms_factor(hidden)
    scaled = (normed * gain).astype(bf16)
    grads = grad_ref[...]
    gw_ref[...] = dot(scaled, grads, 0, 0).astype(bf16)
    grad_normed = dot(grads, wp_ref[:, 0 : plan.qkv], 1, 1)
    for block in range(plan.exp):
        gx_ref[block] = grad_normed[block * plan.tok : (block + 1) * plan.tok].astype(bf16)
    grad_gain = jnp.sum(grad_normed * normed, axis=0, keepdims=True)
    columns = jnp.transpose(jnp.broadcast_to(grad_gain, (plan.chunk, plan.width)))
    by_row = dot(head_ref[...].astype(f32), sums_ref[...], 0, 0, EXACT)
    bias_column = jnp.sum(by_row * spread_ref[...].astype(f32), axis=1, keepdims=True)
    lane = iota((plan.width, plan.chunk), 1)
    small = part_ref[...] + jnp.where(
        lane == place, columns, jnp.where(lane == place + 2, bias_column, 0.0)
    )
    if plan.off:
        small = pltpu.roll(small, plan.chunk - plan.off, axis=1)
    high = small.astype(bf16).astype(f32)
    low = pltpu.roll(small - high, plan.extra, axis=1)
    small_ref[...] = jnp.where(lane < plan.extra, high, low).astype(bf16)


def finish_kernel(plan, gx_ref, gres_ref, x_ref, chunk_ref, out_ref):
    place = plan.off + plan.experts
    gain = jnp.transpose(chunk_ref[...].astype(f32))[place : place + 1, :]
    grad_normed = gx_ref[0].astype(f32)
    for block in range(1, plan.exp):
        grad_normed = grad_normed + gx_ref[block].astype(f32)
    hidden = x_ref[...].astype(f32)
    factor = rms_factor(hidden)
    out_ref[...] = gres_ref[...] + rms_backward(grad_normed, hidden * factor, factor, gain)


def unpack_kernel(plan, got_ref, gq_ref, gk_ref, gv_ref, gwo_ref, small_ref):
    by_exp = []
    for place in range(plan.exp):
        total = got_ref[place].astype(f32)
        for row in range(1, plan.seq):
            total = total + got_ref[row * plan.exp + place].astype(f32)
        by_exp.append(total)
    joined = by_exp[0]
    for total in by_exp[1:]:
        joined = joined + total
    gwo_ref[...] = joined[:, 0 : plan.width]
    small = joined[:, plan.width : plan.width + plan.chunk]
    small_ref[...] = small + pltpu.roll(small, plan.chunk - plan.extra, axis=1)
    start = plan.width + plan.chunk
    for group in range(plan.groups):
        total = by_exp[group * plan.copies]
        for copy in range(1, plan.copies):
            total = total + by_exp[group * plan.copies + copy]
        for number, ref in enumerate((gq_ref, gk_ref, gv_ref)):
            at = start + number * plan.gw
            ref[:, group * plan.gw : (group + 1) * plan.gw] = total[:, at : at + plan.gw]


def call(kernel, plan, in_specs, out, scratch=(), name=None):
    return pl.pallas_call(
        functools.partial(kernel, plan),
        grid=(1,),
        in_specs=in_specs,
        out_specs=[whole(o.shape) for o in out],
        out_shape=out,
        scratch_shapes=list(scratch),
        name=name,
    )


def shaped(*dims, dtype=bf16):
    return jax.ShapeDtypeStruct(dims, dtype)


def body(
    tokens, route_ids, w_query, w_key, w_value, w_output, norm_gains, rel_bias, router,
    w_in, w_out, cotangent,
):
    tok, width = tokens.shape[1:]
    hidden = w_in.shape[2]
    plan = Plan(tok, width, hidden)
    experts = plan.experts
    grid_axes = ("seq", "exp")
    ffn_index = lax.axis_index("ffn")
    swap = [(core, plan.ffn - 1 - core) for core in range(plan.ffn)]

    def exchange(values):
        return lax.all_to_all(values, grid_axes, split_axis=0, concat_axis=0, tiled=True)

    def along(values):
        return lax.all_to_all(values, "exp", split_axis=0, concat_axis=0, tiled=True)

    def partner(values):
        return lax.ppermute(values, "ffn", swap)

    def both_cores(values):
        other = partner(values)
        return jnp.where(
            ffn_index == 0,
            jnp.stack([values, other], axis=1),
            jnp.stack([other, values], axis=1),
        )

    x = tokens[0]
    cot = cotangent[0]
    ids = route_ids[0]
    shard = plan.shard
    bias_column = jnp.pad(rel_bias, (0, shard - plan.bias_shard))[:, None]
    by_group = [
        jnp.transpose(w.reshape(shard, plan.groups, plan.gw), (1, 0, 2))
        for w in (w_query, w_key, w_value)
    ]
    extra = jnp.concatenate([router, norm_gains.T, bias_column], axis=1)
    extra = jnp.pad(extra, ((0, 0), (0, plan.packed - plan.qkv - plan.extra)))
    packed = jnp.concatenate(
        by_group + [jnp.broadcast_to(extra[None], (plan.groups,) + extra.shape)], axis=2
    )
    packed = jnp.broadcast_to(
        packed[None, :, None], (plan.seq, plan.groups, plan.copies, shard, plan.packed)
    ).reshape(experts, shard, plan.packed)
    x_all = along(jnp.broadcast_to(x[None], (plan.exp, tok, width))).reshape(plan.length, width)
    wp = both_cores(exchange(packed)).reshape(width, plan.packed)
    wo = both_cores(
        exchange(jnp.broadcast_to(w_output[None], (experts, shard, width)))
    ).reshape(width, width)
    head_rows, spread = plan.selectors()

    att, qkv, lse, table = call(
        attend_kernel,
        plan,
        [whole(x_all.shape), whole(wp.shape), whole(head_rows.shape), whole(spread.shape)],
        [
            shaped(plan.queries, plan.gw),
            shaped(plan.length, plan.qkv),
            shaped(plan.queries, LANES, dtype=f32),
            shaped(16, LANES, dtype=f32),
        ],
        name="attend",
    )(x_all, wp, head_rows, spread)

    def to_owners(rows):
        blocks = rows.reshape(plan.blocks, tok, plan.gw)
        if plan.copies == 1:
            return blocks
        copy = lax.axis_index("exp") % plan.copies
        mine = jnp.arange(plan.copies) == copy
        return jnp.where(mine[:, None, None, None], blocks[None], 0).reshape(
            plan.exp, tok, plan.gw
        )

    att_recv = along(to_owners(att))
    if plan.copies > 1:
        att_recv = jnp.sum(att_recv.reshape(plan.groups, plan.copies, tok, plan.gw), axis=1)

    send, residual, meta, atok = call(
        middle_kernel,
        plan,
        [
            whole(att_recv.shape), whole(wo.shape), whole(x.shape), whole(cot.shape),
            whole(ids.shape), chunk_spec(plan),
        ],
        [
            shaped(plan.slots, 2 * width),
            shaped(tok, width, dtype=f32),
            shaped(tok, LANES, dtype=f32),
            shaped(tok, width),
        ],
        name="middle",
    )(att_recv, wo, x, cot, ids, wp)

    own = exchange(send.reshape(experts, plan.cap, 2 * width)).reshape(plan.slots, 2 * width)
    other = partner(own)
    block = 512 if hidden % 512 == 0 else hidden
    row_spec = pl.BlockSpec((plan.slots, 2 * width), lambda step: (0, 0))
    in_spec = pl.BlockSpec((1, width, block), lambda step: (0, 0, step))
    out_spec = pl.BlockSpec((1, block, width), lambda step: (0, step, 0))
    mine, theirs, grad_w_in, grad_w_out = pl.pallas_call(
        functools.partial(expert_kernel, plan),
        grid=(hidden // block,),
        in_specs=[row_spec, row_spec, in_spec, out_spec],
        out_specs=[row_spec, row_spec, in_spec, out_spec],
        out_shape=[
            shaped(plan.slots, 2 * width, dtype=f32),
            shaped(plan.slots, 2 * width),
            shaped(1, width, hidden, dtype=f32),
            shaped(1, hidden, width, dtype=f32),
        ],
        scratch_shapes=[
            pltpu.VMEM((2 * plan.slots, 2 * width), bf16),
            pltpu.VMEM((2 * plan.slots, 2 * width), f32),
        ],
        name="experts",
    )(own, other, w_in, w_out)
    total = (mine + partner(theirs).astype(f32)).astype(bf16)
    back = exchange(total.reshape(experts, plan.cap, 2 * width)).reshape(plan.slots, 2 * width)

    output, grad_residual, gatt, gwo, part = call(
        combine_kernel,
        plan,
        [
            whole(back.shape), whole(meta.shape), whole(residual.shape), whole(cot.shape),
            whole(ids.shape), chunk_spec(plan), whole(wo.shape), whole(atok.shape),
        ],
        [
            shaped(tok, width),
            shaped(tok, width, dtype=f32),
            shaped(plan.groups, tok, plan.gw),
            shaped(width, width),
            shaped(width, plan.chunk, dtype=f32),
        ],
        name="combine",
    )(back, meta, residual, cot, ids, wp, wo, atok)

    if plan.copies > 1:
        gatt = jnp.broadcast_to(
            gatt[:, None], (plan.groups, plan.copies, tok, plan.gw)
        ).reshape(plan.exp, tok, plan.gw)
    gatt_recv = along(gatt)
    if plan.copies > 1:
        copy = lax.axis_index("exp") % plan.copies
        gatt_recv = lax.dynamic_slice_in_dim(gatt_recv, copy * plan.blocks, plan.blocks, 0)
    gatt_rows = gatt_recv.reshape(plan.queries, plan.gw)

    gx, gw, small = call(
        backward_kernel,
        plan,
        [
            whole(x_all.shape), whole(wp.shape), whole(head_rows.shape), whole(spread.shape),
            whole(qkv.shape), whole(att.shape), whole(gatt_rows.shape), whole(lse.shape),
            whole(table.shape), whole(part.shape),
        ],
        [
            shaped(plan.exp, tok, width),
            shaped(width, plan.qkv),
            shaped(width, plan.chunk),
        ],
        [
            pltpu.VMEM((plan.length, 2 * plan.gw), f32),
            pltpu.VMEM((plan.length, plan.qkv), bf16),
            pltpu.VMEM((16, LANES), f32),
        ],
        name="backward",
    )(x_all, wp, head_rows, spread, qkv, att, gatt_rows, lse, table, part)

    gx_recv = along(gx)
    grad_tokens = call(
        finish_kernel,
        plan,
        [whole(gx_recv.shape), whole(grad_residual.shape), whole(x.shape), chunk_spec(plan)],
        [shaped(tok, width, dtype=f32)],
        name="finish",
    )(gx_recv, grad_residual, x, wp)[0]

    terms = jnp.concatenate([gwo, small, gw], axis=1).reshape(experts, plan.ffn, shard, -1)
    kept = lax.dynamic_index_in_dim(terms, ffn_index, 1, keepdims=False)
    given = lax.dynamic_index_in_dim(terms, plan.ffn - 1 - ffn_index, 1, keepdims=False)
    joined = (kept.astype(f32) + partner(given).astype(f32)).astype(bf16)
    got = exchange(joined)
    weight = shaped(shard, width, dtype=f32)
    gq, gk, gv, grad_w_output, sums = call(
        unpack_kernel,
        plan,
        [whole(got.shape)],
        [weight] * 4 + [shaped(shard, plan.chunk, dtype=f32)],
        name="unpack",
    )(got)
    return (
        output[None],
        grad_tokens[None],
        gq,
        gk,
        gv,
        grad_w_output,
        sums[:, experts : experts + 2].T,
        sums[: plan.bias_shard, experts + 2],
        sums[:, :experts],
        grad_w_in,
        grad_w_out,
    )


def solution(mesh):
    rows = P(("seq", "ffn"), "exp", None)
    shard = P(("seq", "exp", "ffn"), None)
    gains = P(None, ("seq", "exp", "ffn"))
    bias = P(("seq", "exp", "ffn"))
    hidden_last = P(("seq", "exp"), None, "ffn")
    hidden_first = P(("seq", "exp"), "ffn", None)
    return jax.shard_map(
        body,
        mesh=mesh,
        in_specs=(
            rows, rows, shard, shard, shard, shard, gains, bias, shard, hidden_last, hidden_first, rows,
        ),
        out_specs=(
            rows, rows, shard, shard, shard, shard, gains, bias, shard, hidden_last, hidden_first,
        ),
        check_vma=False,
    )
```

time: 2410 us -> 311 us (0.13)
  waiting for transfers between devices: 1070 us -> 83.1 us
  blocking collectives: 839 us -> 127 us
  local copies, waits for them, and re-layouts: 365 us -> 18.9 us
  matrix products: 61.9 us -> 0 us
  Pallas kernels: 0 us -> 52.5 us
    reduce_scatter x5 -> x0, waiting for transfers between devices: 884 us -> none  [the longest x1 543 us: body(): lax.psum_scatter(result_state[2].astype(jnp.bfloat16), 'exp', scatter_dim...]
    all_to_all x5 -> x4, blocking collectives: 619 us -> 127 us  [exchange(): lax.all_to_all(values, grid_axes, split_axis=0, concat_axis=0, tiled=True)]
    gather x9 -> x0, local copies, waits for them, and re-layouts: 333 us -> none  [the longest x2 204 us: score_block(): jnp.take(bucket_table, jnp.clip(distance, 0, bucket_table.shape[0] - 1),...]
    all_gather x2 -> x0, blocking collectives: 141 us -> none  [the longest x1 97.4 us: fetch_weights(): lax.all_gather(router, ('seq', 'exp', 'ffn'), axis=0, tiled=True)]
    all_gather x5 -> x0, waiting for transfers between devices: 102 us -> none  [the longest x1 54.1 us: fetch_weights(): lax.all_gather(w_value, ('seq', 'exp', 'ffn'), axis=0, tiled=True)]
    unnamed x2 -> x0, blocking collectives: 78.6 us -> none
    dot_general x31 -> x0, matrix products: 61.9 us -> none  [the longest x23 58.4 us: matmul(): return jnp.dot(left, right, preferred_element_type=jnp.float32)]
    pallas_call x0 -> x7, Pallas kernels: none -> 52.5 us  [the longest x1 21.9 us: body(): pl.pallas_call(functools.partial(expert_kernel, plan), grid=(hidden // bl...]
  transfers between devices with their start and end apart: 15 -> 10, of which waited for: 12 -> 8; matrix products, arithmetic and copies ran while one was open for 9% -> 2% of each run, Pallas kernels for 0% -> 2%
where the time goes in v1:
time: 311 us; the launch traced here: 310 us
  blocking collectives  127 us (41%)
  waiting for transfers between devices  83.1 us (27%)
  Pallas kernels  52.5 us (17%)
  local copies, waits for them, and re-layouts  18.9 us (6%)
  starting transfers between devices  18.3 us (6%)
  other arithmetic  9.76 us (3%)
    all_to_all x4, blocking collectives, exchange(): lax.all_to_all(values, grid_axes, split_axis=0, concat_axis=0, tiled=True)  127 us
    all_to_all x4, waiting for transfers between devices, along(): lax.all_to_all(values, 'exp', split_axis=0, concat_axis=0, tiled=True)  46.9 us
    all_to_all x1, waiting for transfers between devices, exchange(): lax.all_to_all(values, grid_axes, split_axis=0, concat_axis=0, tiled=True)  27.9 us
    pallas_call x1, Pallas kernels, body(): pl.pallas_call(functools.partial(expert_kernel, plan), grid=(hidden // bl...  21.9 us
    all_to_all x4, starting transfers between devices, along(): lax.all_to_all(values, 'exp', split_axis=0, concat_axis=0, tiled=True)  13.9 us
    pallas_call x1, Pallas kernels, body(): call(backward_kernel, plan, [whole(x_all.shape), whole(wp.shape), whole(h...  11.3 us
    ppermute x5, waiting for transfers between devices, partner(): return lax.ppermute(values, 'ffn', swap)  8.25 us
  transfers between devices with their start and end apart: 10, of which 8 were waited for; matrix products, arithmetic and copies ran while one was open for 2% of the time, Pallas kernels for 2%

profile of v1, /device:TPU:0, one launch (start us, length us, event | category | flops | bytes accessed | tf_op | source)
XLA Modules:
  0.0 310.0 jit_solution(17203112670950950257)
XLA Ops:
  0.6 0.0 copy-start.7
  0.7 0.9 reshape.75
  1.5 0.9 reshape.76
  2.4 0.9 reshape.77
  3.3 0.7 pad_bitcast_fusion
  4.0 0.7 pad_maximum_fusion.2
  4.7 0.1 copy.47
  4.8 0.1 pad_maximum_fusion.1
  4.9 0.0 copy-start.4
  5.0 23.8 %all_to_all.45 = bf16[16,24,640]{2,1,0:T(8,128)(2,1)S(1)} all-to-all(bf16[16,24,640]{2,1,0:T(8,128)(2,1)S(1)} %bitcast.53), channel_id=1, replica_groups=mesh['seq'=4,'exp'=4,'ffn'=2] {'seq','exp'}, dimensions={0} | all-to-all | bytes 983040 | tf_op jit(solution)/shard_map/all_to_all | solution.py:454
  28.8 0.0 copy-done.7
  28.8 19.9 %all_to_all.46 = bf16[16,24,768]{2,1,0:T(8,128)(2,1)S(1)} all-to-all(bf16[16,24,768]{2,1,0:T(8,128)(2,1)S(1)} %broadcast_in_dim.42), channel_id=1, replica_groups=mesh['seq'=4,'exp'=4,'ffn'=2] {'seq','exp'}, dimensions={0} | all-to-all | bytes 1179648 | tf_op jit(solution)/shard_map/all_to_all | solution.py:454
  48.7 0.0 copy-done.4
  48.7 0.9 broadcast_in_dim.37
  49.6 3.5 %all-to-all-start = ((bf16[4,128,768]{2,1,0:T(8,128)(2,1)}), bf16[4,128,768]{2,1,0:T(8,128)(2,1)S(1)}, u32[]{:S(2)}, u32[]{:S(2)}) async-start(bf16[4,128,768]{2,1,0:T(8,128)(2,1)} %broadcast_in_dim.37), calls=%async_computation | async-start | bytes 1572864 | tf_op jit(solution)/shard_map/all_to_all | solution.py:457
  53.1 0.1 collective-permute-start
  53.2 0.5 collective-permute-start.1
  53.7 1.4 collective-permute-done
  55.1 1.2 maximum_select_fusion.1
  56.3 16.2 %all-to-all-done = bf16[4,128,768]{2,1,0:T(8,128)(2,1)S(1)} async-done(((bf16[4,128,768]{2,1,0:T(8,128)(2,1)}), bf16[4,128,768]{2,1,0:T(8,128)(2,1)S(1)}, u32[]{:S(2)}, u32[]{:S(2)}) %all-to-all-start) | async-done | bytes 786464 | tf_op jit(solution)/shard_map/all_to_all | solution.py:457
  72.5 0.9 copy-done
  73.4 5.1 %attend.1 = (bf16[512,192]{1,0:T(8,128)(2,1)}, bf16[512,576]{1,0:T(8,128)(2,1)}, f32[512,128]{1,0:T(8,128)}, f32[16,128]{1,0:T(8,128)}) custom-call(bf16[512,768]{1,0:T(8,128)(2,1)} %bitcast.45, bf16[768,640]{1,0:T(8,128)(2,1)} %bitcast.36, bf16[16,768]{1,0:T(8,128)(2,1)} %constant.23.clone.head_ref, bf16[768,128]{1,0:T(8,128)(2,1)} %constant.24.clone.spread_ref), custom_call_target="tpu_custom_call" | custom-call | tf_op jit(solution)/shard_map/attend/pallas_call | solution.py:494
  78.5 1.8 copy.38
  80.2 3.4 %all-to-all-start.2 = ((bf16[4,128,192]{1,2,0:T(8,128)(2,1)}), bf16[4,128,192]{1,2,0:T(8,128)(2,1)S(1)}, u32[]{:S(2)}, u32[]{:S(2)}) async-start(bf16[4,128,192]{1,2,0:T(8,128)(2,1)} %copy.38), calls=%async_computation.2 | async-start | bytes 393216 | tf_op jit(solution)/shard_map/all_to_all | solution.py:457
  83.6 0.0 copy-done.8
  83.6 0.7 copy.39
  84.4 0.0 collective-permute-done.1
  84.4 1.2 maximum_select_fusion
  85.6 5.3 %all-to-all-done.2 = bf16[4,128,192]{1,2,0:T(8,128)(2,1)S(1)} async-done(((bf16[4,128,192]{1,2,0:T(8,128)(2,1)}), bf16[4,128,192]{1,2,0:T(8,128)(2,1)S(1)}, u32[]{:S(2)}, u32[]{:S(2)}) %all-to-all-start.2) | async-done | bytes 196640 | tf_op jit(solution)/shard_map/all_to_all | solution.py:457
  90.9 0.8 copy.40.att_ref
  91.7 4.6 %middle.1 = (bf16[512,1536]{1,0:T(8,128)(2,1)}, f32[128,768]{1,0:T(8,128)}, f32[128,128]{1,0:T(8,128)}, bf16[128,768]{1,0:T(8,128)(2,1)}) custom-call(bf16[4,128,192]{2,1,0:T(8,128)(2,1)} %copy.40.att_ref, bf16[768,768]{1,0:T(8,128)(2,1)} %bitcast.41, bf16[128,768]{1,0:T(8,128)(2,1)} %bitcast.54, bf16[128,768]{1,0:T(8,128)(2,1)} %bitcast.60, ...), custom_call_target="tpu_custom_call" | custom-call | tf_op jit(solution)/shard_map/middle/pallas_call | solution.py:521
  96.3 40.4 %all_to_all.47 = bf16[16,32,1536]{2,1,0:T(8,128)(2,1)S(1)} all-to-all(bf16[16,32,1536]{2,1,0:T(8,128)(2,1)} %bitcast.57), channel_id=1, replica_groups=mesh['seq'=4,'exp'=4,'ffn'=2] {'seq','exp'}, dimensions={0} | all-to-all | bytes 3145728 | tf_op jit(solution)/shard_map/all_to_all | solution.py:454
  136.7 0.0 collective-permute-start.2
  136.7 3.4 %collective-permute-done.2.other_ref = bf16[512,1536]{1,0:T(8,128)(2,1)S(1)} collective-permute-done((bf16[512,1536]{1,0:T(8,128)(2,1)S(1)}, bf16[512,1536]{1,0:T(8,128)(2,1)S(1)}, u32[]{:S(2)}, u32[]{:S(2)}) %collective-permute-start.2) | collective-permute-done | bytes 1572896 | tf_op jit(solution)/shard_map/ppermute | solution.py:460
  140.1 0.0 copy-done.1
  140.1 1.2 copy-done.5
  141.3 21.9 %experts.1 = (f32[512,1536]{1,0:T(8,128)}, bf16[512,1536]{1,0:T(8,128)(2,1)}, f32[1,768,1536]{2,1,0:T(8,128)}, f32[1,1536,768]{2,1,0:T(8,128)}) custom-call(bf16[512,1536]{1,0:T(8,128)(2,1)} %bitcast.50, bf16[512,1536]{1,0:T(8,128)(2,1)} %copy-done.5, bf16[1,768,1536]{2,1,0:T(8,128)(2,1)} %win_ref.1, bf16[1,1536,768]{2,1,0:T(8,128)(2,1)} %wout_ref.1), custom_call_target="tpu_custom_call" | custom-call | tf_op jit(solution)/shard_map/experts/pallas_call | solution.py:543
  163.3 0.1 collective-permute-start.3
  163.4 3.5 %collective-permute-done.3 = bf16[512,1536]{1,0:T(8,128)(2,1)S(1)} collective-permute-done((bf16[512,1536]{1,0:T(8,128)(2,1)}, bf16[512,1536]{1,0:T(8,128)(2,1)S(1)}, u32[]{:S(2)}, u32[]{:S(2)}) %collective-permute-start.3) | collective-permute-done | bytes 1572896 | tf_op jit(solution)/shard_map/ppermute | solution.py:460
  166.9 2.5 add_convert_fusion
  169.3 42.5 %all_to_all.48 = bf16[16,32,1536]{2,1,0:T(8,128)(2,1)} all-to-all(bf16[16,32,1536]{2,1,0:T(8,128)(2,1)S(1)} %bitcast.48), channel_id=1, replica_groups=mesh['seq'=4,'exp'=4,'ffn'=2] {'seq','exp'}, dimensions={0} | all-to-all | bytes 3145728 | tf_op jit(solution)/shard_map/all_to_all | solution.py:454
  211.9 5.1 %combine.1 = (bf16[128,768]{1,0:T(8,128)(2,1)}, f32[128,768]{1,0:T(8,128)}, bf16[4,128,192]{2,1,0:T(8,128)(2,1)}, bf16[768,768]{1,0:T(8,128)(2,1)}, f32[768,128]{1,0:T(8,128)}) custom-call(bf16[512,1536]{1,0:T(8,128)(2,1)} %bitcast.47, f32[128,128]{1,0:T(8,128)} %get-tuple-element.40.meta_ref, f32[128,768]{1,0:T(8,128)} %get-tuple-element.41.res_ref, ...), custom_call_target="tpu_custom_call" | custom-call | tf_op jit(solution)/shard_map/combine/pallas_call | solution.py:563
  217.0 1.8 copy.41
  218.8 3.6 %all-to-all-start.6 = ((bf16[4,128,192]{1,2,0:T(8,128)(2,1)}), bf16[4,128,192]{1,2,0:T(8,128)(2,1)S(1)}, u32[]{:S(2)}, u32[]{:S(2)}) async-start(bf16[4,128,192]{1,2,0:T(8,128)(2,1)} %copy.41), calls=%async_computation.6 | async-start | bytes 393216 | tf_op jit(solution)/shard_map/all_to_all | solution.py:457
  222.4 7.0 %all-to-all-done.6 = bf16[4,128,192]{1,2,0:T(8,128)(2,1)S(1)} async-done(((bf16[4,128,192]{1,2,0:T(8,128)(2,1)}), bf16[4,128,192]{1,2,0:T(8,128)(2,1)S(1)}, u32[]{:S(2)}, u32[]{:S(2)}) %all-to-all-start.6) | async-done | bytes 196640 | tf_op jit(solution)/shard_map/all_to_all | solution.py:457
  229.4 0.8 copy.42
  230.3 11.3 %backward.1 = (bf16[4,128,768]{2,1,0:T(8,128)(2,1)}, bf16[768,576]{1,0:T(8,128)(2,1)}, bf16[768,128]{1,0:T(8,128)(2,1)}) custom-call(bf16[512,768]{1,0:T(8,128)(2,1)} %bitcast.46, bf16[768,640]{1,0:T(8,128)(2,1)} %bitcast.39, bf16[16,768]{1,0:T(8,128)(2,1)} %constant.23.clone.head_ref, bf16[768,128]{1,0:T(8,128)(2,1)} %constant.24.clone.spread_ref, ...), custom_call_target="tpu_custom_call" | custom-call | tf_op jit(solution)/shard_map/backward/pallas_call | solution.py:590
  241.5 0.0 copy-done.6
  241.5 1.4 pad_maximum_fusion
  243.0 1.1 dynamic-slice_bitcast_fusion
  244.1 0.0 collective-permute-start.4
  244.1 3.5 %all-to-all-start.7 = ((bf16[4,128,768]{2,1,0:T(8,128)(2,1)}), bf16[4,128,768]{2,1,0:T(8,128)(2,1)S(1)}, u32[]{:S(2)}, u32[]{:S(2)}) async-start(bf16[4,128,768]{2,1,0:T(8,128)(2,1)} %get-tuple-element.49), calls=%async_computation.7 | async-start | bytes 1572864 | tf_op jit(solution)/shard_map/all_to_all | solution.py:457
  247.6 0.0 collective-permute-done.4
  247.6 2.6 fusion
  250.3 18.4 %all-to-all-done.7.gx_ref = bf16[4,128,768]{2,1,0:T(8,128)(2,1)S(1)} async-done(((bf16[4,128,768]{2,1,0:T(8,128)(2,1)}), bf16[4,128,768]{2,1,0:T(8,128)(2,1)S(1)}, u32[]{:S(2)}, u32[]{:S(2)}) %all-to-all-start.7) | async-done | bytes 786464 | tf_op jit(solution)/shard_map/all_to_all | solution.py:457
  268.6 3.7 %all-to-all-start.8 = ((bf16[16,24,1472]{2,1,0:T(8,128)(2,1)}), bf16[16,24,1472]{2,1,0:T(8,128)(2,1)S(1)}, u32[]{:S(2)}, u32[]{:S(2)}) async-start(bf16[16,24,1472]{2,1,0:T(8,128)(2,1)} %fusion), calls=%async_computation.8 | async-start | bytes 2359296 | tf_op jit(solution)/shard_map/all_to_all | solution.py:454
  272.4 2.4 finish.1
  274.8 27.9 %all-to-all-done.8.got_ref = bf16[16,24,1472]{2,1,0:T(8,128)(2,1)S(1)} async-done(((bf16[16,24,1472]{2,1,0:T(8,128)(2,1)}), bf16[16,24,1472]{2,1,0:T(8,128)(2,1)S(1)}, u32[]{:S(2)}, u32[]{:S(2)}) %all-to-all-start.8) | async-done | bytes 1130528 | tf_op jit(solution)/shard_map/all_to_all | solution.py:454
  302.7 1.0 copy-done.2
  303.7 2.1 unpack.1
  305.8 0.8 slice_bitcast_fusion
  306.6 1.4 slice_reduce_fusion
  308.0 0.6 copy.44
  308.6 1.4 copy.45
  (13 shorter events, 0.1 us)
Async XLA Ops:
  0.6 28.1 %copy-start.7 = (bf16[24,768]{1,0:T(8,128)(2,1)S(1)}, bf16[24,768]{1,0:T(8,128)(2,1)}, u32[]{:S(2)}) copy-start(bf16[24,768]{1,0:T(8,128)(2,1)} %param.19) | copy-start | bytes 110596
  4.9 43.8 %copy-start.4 = (bf16[1,128,768]{2,1,0:T(8,128)(2,1)S(1)}, bf16[1,128,768]{2,1,0:T(8,128)(2,1)}, u32[]{:S(2)}) copy-start(bf16[1,128,768]{2,1,0:T(8,128)(2,1)} %param.14) | copy-start | bytes 589828
  49.6 22.8 %all-to-all-start = ((bf16[4,128,768]{2,1,0:T(8,128)(2,1)}), bf16[4,128,768]{2,1,0:T(8,128)(2,1)S(1)}, u32[]{:S(2)}, u32[]{:S(2)}) async-start(bf16[4,128,768]{2,1,0:T(8,128)(2,1)} %broadcast_in_dim.37), calls=%async_computation | async-start | bytes 1572864 | tf_op jit(solution)/shard_map/all_to_all | solution.py:457
  53.1 1.9 collective-permute-start
  53.2 31.1 %collective-permute-start.1 = (bf16[16,24,768]{2,1,0:T(8,128)(2,1)S(1)}, bf16[16,24,768]{2,1,0:T(8,128)(2,1)S(1)}, u32[]{:S(2)}, u32[]{:S(2)}) collective-permute-start(bf16[16,24,768]{2,1,0:T(8,128)(2,1)S(1)} %all_to_all.46), channel_id=1, source_target_pairs={{0,1},{1,0},{2,3},{3,2},{4,5},{5,4},{6,7},{7,6},{8,9},{9,8},{10,11... | collective-permute-start | bytes 1769480 | tf_op jit(solution)/shard_map/ppermute | solution.py:460
  56.3 27.4 %copy-start.8 = (s32[1,128,2]{1,2,0:T(2,128)S(1)}, s32[1,128,2]{1,2,0:T(2,128)}, u32[]{:S(2)}) copy-start(s32[1,128,2]{1,2,0:T(2,128)} %param.15) | copy-start | bytes 3076
  72.5 0.9 copy-start
  80.2 10.6 %all-to-all-start.2 = ((bf16[4,128,192]{1,2,0:T(8,128)(2,1)}), bf16[4,128,192]{1,2,0:T(8,128)(2,1)S(1)}, u32[]{:S(2)}, u32[]{:S(2)}) async-start(bf16[4,128,192]{1,2,0:T(8,128)(2,1)} %copy.38), calls=%async_computation.2 | async-start | bytes 393216 | tf_op jit(solution)/shard_map/all_to_all | solution.py:457
  136.7 3.4 %copy-start.1 = (bf16[16,32,1536]{2,1,0:T(8,128)(2,1)}, bf16[16,32,1536]{2,1,0:T(8,128)(2,1)S(1)}, u32[]{:S(2)}) copy-start(bf16[16,32,1536]{2,1,0:T(8,128)(2,1)S(1)} %all_to_all.47) | copy-start | bytes 4718596
  136.7 3.4 %collective-permute-start.2 = (bf16[512,1536]{1,0:T(8,128)(2,1)S(1)}, bf16[512,1536]{1,0:T(8,128)(2,1)S(1)}, u32[]{:S(2)}, u32[]{:S(2)}) collective-permute-start(bf16[512,1536]{1,0:T(8,128)(2,1)S(1)} %bitcast.49), channel_id=1, source_target_pairs={{0,1},{1,0},{2,3},{3,2},{4,5},{5,4},{6,7},{7,6},{8,9},{9,8},{10,11... | collective-permute-start | bytes 4718600 | tf_op jit(solution)/shard_map/ppermute | solution.py:460
  140.1 1.2 copy-start.5
  163.3 3.6 %collective-permute-start.3 = (bf16[512,1536]{1,0:T(8,128)(2,1)}, bf16[512,1536]{1,0:T(8,128)(2,1)S(1)}, u32[]{:S(2)}, u32[]{:S(2)}) collective-permute-start(bf16[512,1536]{1,0:T(8,128)(2,1)} %get-tuple-element.39), channel_id=1, source_target_pairs={{0,1},{1,0},{2,3},{3,2},{4,5},{5,4},{6,7},{7,6},{8,9},{9,8},{10,11... | collective-permute-start | bytes 4718600 | tf_op jit(solution)/shard_map/ppermute | solution.py:460
  218.8 10.6 %all-to-all-start.6 = ((bf16[4,128,192]{1,2,0:T(8,128)(2,1)}), bf16[4,128,192]{1,2,0:T(8,128)(2,1)S(1)}, u32[]{:S(2)}, u32[]{:S(2)}) async-start(bf16[4,128,192]{1,2,0:T(8,128)(2,1)} %copy.41), calls=%async_computation.6 | async-start | bytes 393216 | tf_op jit(solution)/shard_map/all_to_all | solution.py:457
  230.3 11.3 %copy-start.6 = (bf16[768,768]{1,0:T(8,128)(2,1)S(1)}, bf16[768,768]{1,0:T(8,128)(2,1)}, u32[]{:S(2)}) copy-start(bf16[768,768]{1,0:T(8,128)(2,1)} %get-tuple-element.51) | copy-start | bytes 3538948
  244.1 3.5 %collective-permute-start.4 = (bf16[16,24,1472]{2,1,0:T(8,128)(2,1)}, bf16[16,24,1472]{2,1,0:T(8,128)(2,1)}, u32[]{:S(2)}, u32[]{:S(2)}) collective-permute-start(bf16[16,24,1472]{2,1,0:T(8,128)(2,1)} %dynamic-slice_bitcast_fusion), channel_id=1, source_target_pairs={{0,1},{1,0},{2,3},{3,2},{4,5},{5,4},{6,7},{7,6},{8,9},{9,8},{10,11... | collective-permute-start | bytes 3391496 | tf_op jit(solution)/shard_map/ppermute | solution.py:460
  244.1 24.5 %all-to-all-start.7 = ((bf16[4,128,768]{2,1,0:T(8,128)(2,1)}), bf16[4,128,768]{2,1,0:T(8,128)(2,1)S(1)}, u32[]{:S(2)}, u32[]{:S(2)}) async-start(bf16[4,128,768]{2,1,0:T(8,128)(2,1)} %get-tuple-element.49), calls=%async_computation.7 | async-start | bytes 1572864 | tf_op jit(solution)/shard_map/all_to_all | solution.py:457
  268.6 3.7 %copy-start.3 = (bf16[4,128,768]{2,1,0:T(8,128)(2,1)}, bf16[4,128,768]{2,1,0:T(8,128)(2,1)S(1)}, u32[]{:S(2)}) copy-start(bf16[4,128,768]{2,1,0:T(8,128)(2,1)S(1)} %all-to-all-done.7.gx_ref) | copy-start | bytes 2359300
  268.6 34.0 %all-to-all-start.8 = ((bf16[16,24,1472]{2,1,0:T(8,128)(2,1)}), bf16[16,24,1472]{2,1,0:T(8,128)(2,1)S(1)}, u32[]{:S(2)}, u32[]{:S(2)}) async-start(bf16[16,24,1472]{2,1,0:T(8,128)(2,1)} %fusion), calls=%async_computation.8 | async-start | bytes 2359296 | tf_op jit(solution)/shard_map/all_to_all | solution.py:454
  302.7 1.0 copy-start.2
